TPU v7x, 256 devices: a whole 4x4x8 slice. The times are simulated.
256 devices in a mesh: dp: 8 (over y, core), ctx: 32 (over x, z).
Axes of the slice: x: 4, y: 4, z: 8, core: 2. Of those that a mesh axis runs over, the one named last changes fastest.
Arguments:
- features: bfloat16 [8, 4096, 1536], P('dp', 'ctx'), may hold values from -6 to 6
- short_weight: float32 [7, 1536], replicated, may hold values from -2 to 2
- long_filter: float32 [4096, 512], P('ctx'), may hold values from -4 to 4
- skip_bias: float32 [512], replicated, may hold values from 0.5 to 1.5
- cotangent: bfloat16 [8, 4096, 512], P('dp', 'ctx'), may hold values from -6 to 6
Outputs:
- layer_out: bfloat16 [8, 4096, 512], P('dp', 'ctx')
- grad_features: bfloat16 [8, 4096, 1536], P('dp', 'ctx')
- grad_short: float32 [7, 1536], replicated
- grad_filter: float32 [4096, 512], P('ctx')
- grad_skip: float32 [512], replicated
All inputs are finite; a program needn't handle non-finite values.
Results may differ from a plain program's by a relative error of at most 0.001.
Values may be sent and summed in bfloat16 or wider, within the bound.
A program may use at most 64 MiB of HBM per device.

v0:
```python
import math
import jax
import jax.numpy as jnp
from jax import lax
from jax.sharding import PartitionSpec as P

PRECISE = lax.Precision.HIGHEST


def swapped(value, axis, distance):
    mask = 2**distance
    pairs = [(source, source ^ mask) for source in range(lax.axis_size(axis))]
    return lax.ppermute(value, axis, pairs)


def shifted(value, axis, steps):
    count = lax.axis_size(axis)
    initial, last = (max(0, -steps), min(count, count - steps))
    return lax.ppermute(value, axis, [(source, source + steps) for source in range(initial, last)])


def bit_reverse(index_value, bit_count):
    reversed_value = jnp.zeros_like(index_value)
    for bit_place in range(bit_count):
        digit_now = index_value // 2**bit_place % 2
        reversed_value = reversed_value + digit_now * 2 ** (bit_count - 1 - bit_place)
    return reversed_value


def spectral_table(device, parts_count, tokens):
    bit_count = parts_count.bit_length() - 1
    coarse_freq = 2 * bit_reverse(device, bit_count) + jnp.arange(2, dtype=jnp.int32)
    total_points = 2 * parts_count * tokens
    column_index = jnp.arange(tokens, dtype=jnp.int32)
    full_freq = coarse_freq[:, None] + 2 * parts_count * column_index[None, :]
    phase_value = column_index[None, None, :] * full_freq[:, :, None] % total_points
    angle_value = phase_value.astype(jnp.float32) * (2.0 * math.pi / total_points)
    return (jnp.cos(angle_value), -jnp.sin(angle_value))


def contract(matrix, values):
    return jnp.einsum("akm,amw->akw", matrix, values, precision=PRECISE)


def contract_back(matrix, values):
    return jnp.einsum("akm,akw->amw", matrix, values, precision=PRECISE)


def local_forward(spec_real, spec_imag, table):
    table_real, table_imag = table
    out_real = contract(table_real, spec_real) - contract(table_imag, spec_imag)
    out_imag = contract(table_real, spec_imag) + contract(table_imag, spec_real)
    return (out_real, out_imag)


def local_inverse(spec_real, spec_imag, table):
    table_real, table_imag = table
    factor = 1.0 / spec_real.shape[1]
    out_real = (
        contract_back(table_real, spec_real) + contract_back(table_imag, spec_imag)
    ) * factor
    out_imag = (
        contract_back(table_real, spec_imag) - contract_back(table_imag, spec_real)
    ) * factor
    return (out_real, out_imag)


def pair_swap(stacked, bit_place):
    return swapped(stacked, "ctx", bit_place)


def pair_swap_back(stacked, bit_place):
    return swapped(stacked, "ctx", bit_place)


def section_terms(device, bit_place):
    span_size = 2**bit_place
    upper_flag = device // span_size % 2
    sign_value = (1 - 2 * upper_flag).astype(jnp.float32)
    turn_value = math.pi / span_size * (upper_flag * (device % span_size)).astype(jnp.float32)
    return (sign_value, jnp.cos(turn_value), jnp.sin(turn_value))


def butterfly_forward(signals):
    parts_count = lax.axis_size("ctx")
    device = lax.axis_index("ctx")
    bit_count = parts_count.bit_length() - 1
    angle_value = math.pi * device.astype(jnp.float32) / parts_count
    spec_real = jnp.stack([signals, signals * jnp.cos(angle_value)])
    spec_imag = jnp.stack([jnp.zeros_like(signals), -signals * jnp.sin(angle_value)])
    for bit_place in reversed(range(bit_count)):
        sign_value, cos_turn, sin_turn = section_terms(device, bit_place)
        partner = pair_swap(jnp.stack([spec_real, spec_imag]), bit_place)
        joined_real = partner[0] + sign_value * spec_real
        joined_imag = partner[1] + sign_value * spec_imag
        spec_real = joined_real * cos_turn + joined_imag * sin_turn
        spec_imag = joined_imag * cos_turn - joined_real * sin_turn
    return (spec_real, spec_imag)


def butterfly_inverse(spec_real, spec_imag):
    parts_count = lax.axis_size("ctx")
    device = lax.axis_index("ctx")
    bit_count = parts_count.bit_length() - 1
    for bit_place in range(bit_count):
        sign_value, cos_turn, sin_turn = section_terms(device, bit_place)
        turned_real = spec_real * cos_turn - spec_imag * sin_turn
        turned_imag = spec_imag * cos_turn + spec_real * sin_turn
        partner = pair_swap_back(jnp.stack([turned_real, turned_imag]), bit_place)
        spec_real = 0.5 * (partner[0] + sign_value * turned_real)
        spec_imag = 0.5 * (partner[1] + sign_value * turned_imag)
    angle_value = math.pi * device.astype(jnp.float32) / parts_count
    cos_last = jnp.cos(angle_value)
    sin_last = jnp.sin(angle_value)
    out_real = 0.5 * (spec_real[0] + spec_real[1] * cos_last - spec_imag[1] * sin_last)
    out_imag = 0.5 * (spec_imag[0] + spec_imag[1] * cos_last + spec_real[1] * sin_last)
    return (out_real, out_imag)


def per_device(features, short_weight, long_filter, skip_bias, cotangent):
    taps = short_weight.shape[0]
    token_rows = features[0]
    tokens = token_rows.shape[0]
    channels = long_filter.shape[1]
    parts_count = lax.axis_size("ctx")
    device = lax.axis_index("ctx")
    history = shifted(token_rows[tokens - (taps - 1) :], "ctx", 1)
    extended = jnp.concatenate([history, token_rows], axis=0).astype(jnp.float32)
    mixed_feats = jnp.zeros((tokens, token_rows.shape[1]), jnp.float32)
    for tap_index in range(taps):
        start_row = taps - 1 - tap_index
        mixed_feats = (
            mixed_feats + short_weight[tap_index] * extended[start_row : start_row + tokens]
        )
    query = mixed_feats[:, :channels]
    key_part = mixed_feats[:, channels : 2 * channels]
    value_part = mixed_feats[:, 2 * channels :]
    gated = key_part * value_part
    upstream = cotangent[0].astype(jnp.float32)
    dconv = upstream * query
    signals = jnp.concatenate([gated, long_filter, dconv], axis=1)
    table = spectral_table(device, parts_count, tokens)
    spec_real, spec_imag = butterfly_forward(signals)
    spec_real, spec_imag = local_forward(spec_real, spec_imag, table)
    gated_real = spec_real[..., :channels]
    gated_imag = spec_imag[..., :channels]
    filter_real = spec_real[..., channels : 2 * channels]
    filter_imag = spec_imag[..., channels : 2 * channels]
    dconv_real = spec_real[..., 2 * channels :]
    dconv_imag = spec_imag[..., 2 * channels :]
    conv_real = gated_real * filter_real - gated_imag * filter_imag
    conv_imag = gated_real * filter_imag + gated_imag * filter_real
    back_real = filter_real * dconv_real + filter_imag * dconv_imag
    back_imag = filter_real * dconv_imag - filter_imag * dconv_real
    corr_real = gated_real * dconv_real + gated_imag * dconv_imag
    corr_imag = gated_real * dconv_imag - gated_imag * dconv_real
    inverse_real = jnp.concatenate([conv_real - back_imag, corr_real], axis=-1)
    inverse_imag = jnp.concatenate([conv_imag + back_real, corr_imag], axis=-1)
    inverse_real, inverse_imag = local_inverse(inverse_real, inverse_imag, table)
    result_real, result_imag = butterfly_inverse(inverse_real, inverse_imag)
    long_conv = result_real[:, :channels] + skip_bias * gated
    dgated = result_imag[:, :channels] + skip_bias * dconv
    filter_part = result_real[:, channels:]
    layer_out = (query * long_conv).astype(jnp.bfloat16)[None]
    dmixed = jnp.concatenate([upstream * long_conv, dgated * value_part, dgated * key_part], axis=1)
    later = shifted(dmixed[: taps - 1], "ctx", -1)
    ahead = jnp.concatenate([dmixed, later], axis=0)
    grad_local = jnp.zeros_like(dmixed)
    short_rows = []
    for tap_index in range(taps):
        grad_local = grad_local + short_weight[tap_index] * ahead[tap_index : tap_index + tokens]
        start_row = taps - 1 - tap_index
        short_rows.append(jnp.sum(dmixed * extended[start_row : start_row + tokens], axis=0))
    grad_features = grad_local.astype(jnp.bfloat16)[None]
    short_part = jnp.stack(short_rows)
    skip_part = jnp.sum(dconv * gated, axis=0)
    scale = 1.0 / math.sqrt(lax.axis_size("dp") * parts_count * tokens)
    filter_sum = lax.psum(filter_part, "dp")
    short_sum, skip_sum = lax.psum((short_part, skip_part), ("dp", "ctx"))
    return (layer_out, grad_features, short_sum * scale, filter_sum * scale, skip_sum * scale)


def solution(mesh):
    return jax.shard_map(
        per_device,
        mesh=mesh,
        in_specs=(P("dp", "ctx", None), P(), P("ctx", None), P(), P("dp", "ctx", None)),
        out_specs=(P("dp", "ctx", None), P("dp", "ctx", None), P(), P("ctx", None), P()),
        check_vma=False,
    )
```

profile of v0, /device:TPU:2, one launch (start us, length us, event | category | flops | bytes accessed | tf_op | source)
XLA Modules:
  0.0 1050.0 jit_solution(7923902592177502704)
XLA Ops:
  7.2 0.7 slice_bitcast_fusion.20
  8.0 3.8 collective-permute-start
  11.8 1.3 slice_reduce_fusion.6
  13.2 4.3 collective-permute-done
  17.5 1.1 maximum_convert_fusion
  18.6 0.6 multiply_add_fusion.10
  19.6 1.0 copy-done.15
  21.3 0.5 copy-done.11
  22.0 1.9 pad_maximum_fusion
  23.9 2.4 collective-permute-start.1
  26.5 68.2 %collective-permute-done.1 = f32[2,2,128,1536]{3,2,1,0:T(8,128)} collective-permute-done((f32[2,2,128,1536]{3,2,1,0:T(8,128)}, f32[2,2,128,1536]{3,2,1,0:T(8,128)}, u32[]{:S(2)}, u32[]{:S(2)}) %collective-permute-start.1) | collective-permute-done | bytes 3145760 | tf_op jit(solution)/shard_map/ppermute | solution.py:13
  94.7 3.0 multiply_subtract_fusion.4
  97.7 2.0 pad_maximum_fusion.1
  100.3 67.9 %collective-permute-done.2 = f32[2,2,128,1536]{3,2,1,0:T(8,128)} collective-permute-done((f32[2,2,128,1536]{3,2,1,0:T(8,128)}, f32[2,2,128,1536]{3,2,1,0:T(8,128)}, u32[]{:S(2)}, u32[]{:S(2)}) %collective-permute-start.2) | collective-permute-done | bytes 3145760 | tf_op jit(solution)/shard_map/ppermute | solution.py:13
  168.2 3.1 multiply_subtract_fusion.3
  171.3 2.1 pad_maximum_fusion.2
  174.0 4.0 collective-permute-start.3
  178.1 135.4 %collective-permute-done.3 = f32[2,2,128,1536]{3,2,1,0:T(8,128)} collective-permute-done((f32[2,2,128,1536]{3,2,1,0:T(8,128)}, f32[2,2,128,1536]{3,2,1,0:T(8,128)}, u32[]{:S(2)}, u32[]{:S(2)}) %collective-permute-start.3) | collective-permute-done | bytes 3145760 | tf_op jit(solution)/shard_map/ppermute | solution.py:13
  313.5 3.6 multiply_subtract_fusion.2
  317.1 2.1 pad_maximum_fusion.3
  319.4 137.3 %collective-permute-done.4 = f32[2,2,128,1536]{3,2,1,0:T(8,128)} collective-permute-done((f32[2,2,128,1536]{3,2,1,0:T(8,128)}, f32[2,2,128,1536]{3,2,1,0:T(8,128)}, u32[]{:S(2)}, u32[]{:S(2)}) %collective-permute-start.4) | collective-permute-done | bytes 3145760 | tf_op jit(solution)/shard_map/ppermute | solution.py:13
  456.7 3.1 multiply_add_fusion.1
  459.8 2.0 pad_maximum_fusion.4
  461.9 0.6 copy-done.5
  462.6 69.4 %collective-permute-done.5 = f32[2,2,128,1536]{3,2,1,0:T(8,128)} collective-permute-done((f32[2,2,128,1536]{3,2,1,0:T(8,128)}, f32[2,2,128,1536]{3,2,1,0:T(8,128)}, u32[]{:S(2)}, u32[]{:S(2)}) %collective-permute-start.5) | collective-permute-done | bytes 3145760 | tf_op jit(solution)/shard_map/ppermute | solution.py:13
  532.0 3.5 fusion.2
  535.5 2.0 fusion.32
  537.5 2.0 fusion.33
  539.4 2.0 convolution_add_fusion
  541.4 2.0 convolution_subtract_fusion
  544.0 1.5 fusion.24
  545.6 1.7 fusion.23
  547.3 1.5 convolution_add_fusion.1
  548.8 1.5 convolution_subtract_fusion.1
  550.6 1.5 pad_maximum_fusion.5
  552.4 45.8 %collective-permute-done.6 = f32[2,2,128,1024]{3,2,1,0:T(8,128)} collective-permute-done((f32[2,2,128,1024]{3,2,1,0:T(8,128)}, f32[2,2,128,1024]{3,2,1,0:T(8,128)}, u32[]{:S(2)}, u32[]{:S(2)}) %collective-permute-start.6) | collective-permute-done | bytes 2097184 | tf_op jit(solution)/shard_map/ppermute | solution.py:13
  598.2 2.0 multiply_add_fusion.8
  600.5 0.8 copy-done.6
  601.2 1.5 pad_maximum_fusion.6
  602.7 2.1 collective-permute-start.7
  604.8 89.6 %collective-permute-done.7 = f32[2,2,128,1024]{3,2,1,0:T(8,128)} collective-permute-done((f32[2,2,128,1024]{3,2,1,0:T(8,128)}, f32[2,2,128,1024]{3,2,1,0:T(8,128)}, u32[]{:S(2)}, u32[]{:S(2)}) %collective-permute-start.7) | collective-permute-done | bytes 2097184 | tf_op jit(solution)/shard_map/ppermute | solution.py:13
  694.5 2.3 multiply_add_fusion.7
  697.0 0.8 copy-done.7
  698.1 3.7 collective-permute-start.8
  701.8 92.3 %collective-permute-done.8 = f32[2,2,128,1024]{3,2,1,0:T(8,128)} collective-permute-done((f32[2,2,128,1024]{3,2,1,0:T(8,128)S(1)}, f32[2,2,128,1024]{3,2,1,0:T(8,128)}, u32[]{:S(2)}, u32[]{:S(2)}) %collective-permute-start.8) | collective-permute-done | bytes 2097184 | tf_op jit(solution)/shard_map/ppermute | solution.py:13
  794.1 2.7 multiply_add_fusion.6
  796.8 1.5 pad_maximum_fusion.8
  798.3 0.9 collective-permute-start.9
  799.2 46.3 %collective-permute-done.9 = f32[2,2,128,1024]{3,2,1,0:T(8,128)} collective-permute-done((f32[2,2,128,1024]{3,2,1,0:T(8,128)}, f32[2,2,128,1024]{3,2,1,0:T(8,128)}, u32[]{:S(2)}, u32[]{:S(2)}) %collective-permute-start.9) | collective-permute-done | bytes 2097184 | tf_op jit(solution)/shard_map/ppermute | solution.py:13
  845.5 2.0 multiply_subtract_fusion.5
  847.8 3.2 collective-permute-start.10
  851.0 45.0 %collective-permute-done.10 = f32[2,2,128,1024]{3,2,1,0:T(8,128)S(1)} collective-permute-done((f32[2,2,128,1024]{3,2,1,0:T(8,128)S(1)}, f32[2,2,128,1024]{3,2,1,0:T(8,128)S(1)}, u32[]{:S(2)}, u32[]{:S(2)}) %collective-permute-start.10) | collective-permute-done | bytes 2097184 | tf_op jit(solution)/shard_map/ppermute | solution.py:13
  896.0 0.6 fusion.12
  896.9 0.9 copy-done.10
  897.8 1.0 convert_multiply_fusion
  898.8 0.7 multiply_reduce_fusion
  899.7 75.3 %all-reduce.1 = (f32[7,1536]{1,0:T(8,128)S(1)}, f32[512]{0:T(512)S(1)}) all-reduce(f32[7,1536]{1,0:T(8,128)S(1)} %stack.165, f32[512]{0:T(512)S(1)} %get-tuple-element.21), channel_id=1, replica_groups=mesh['dp'=8,'ctx'=32] {'dp','ctx'}, use_global_device_ids=true, to_apply=%region_7.8 | all-reduce | flops 11264 | bytes 90112 | tf_op jit(solution)/shard_map/psum | solution.py:179
  975.1 0.6 broadcast_multiply_fusion.1
  975.7 4.7 collective-permute-start.11
  980.5 0.6 broadcast_multiply_fusion.2
  981.1 1.1 collective-permute-done.11
  982.3 1.4 fusion.41
  983.7 57.8 %all-reduce.4.cloned.1.call-done = f32[128,512]{1,0:T(8,128)} async-done(((f32[128,512]{1,0:T(8,128)}), f32[128,512]{1,0:T(8,128)}) %all-reduce.4.cloned.1.call-update) | async-done | bytes 262160 | tf_op jit(solution)/shard_map/psum | solution.py:178
  1041.4 1.7 broadcast_multiply_fusion
  (62 shorter events, 5.0 us)
Async XLA Ops:
  7.2 1034.3 %all-reduce.4.cloned.1.call-start = ((), (), s32[]{:S(2)}) async-start(), calls=%async_computation | async-start | bytes 524288 | tf_op jit(solution)/shard_map/psum | solution.py:178
  8.0 9.5 collective-permute-start
  18.6 0.9 copy-start.16
  19.5 1.4 copy-start.9
  19.5 1.1 copy-start.15
  19.6 1.3 copy-start.13
  20.9 0.9 copy-start.11
  20.9 1.1 copy-start.12
  23.9 70.8 %collective-permute-start.1 = (f32[2,2,128,1536]{3,2,1,0:T(8,128)}, f32[2,2,128,1536]{3,2,1,0:T(8,128)}, u32[]{:S(2)}, u32[]{:S(2)}) collective-permute-start(f32[2,2,128,1536]{3,2,1,0:T(8,128)} %pad_maximum_fusion), channel_id=1, source_target_pairs={{0,16},{1,17},{2,18},{3,19},{4,20},{5,21},{6,22},{7,23},{8,24},{9,... | collective-permute-start | bytes 9437192 | tf_op jit(solution)/shard_map/ppermute | solution.py:13
  97.7 2.1 copy-start.1
  99.8 68.4 %collective-permute-start.2 = (f32[2,2,128,1536]{3,2,1,0:T(8,128)}, f32[2,2,128,1536]{3,2,1,0:T(8,128)}, u32[]{:S(2)}, u32[]{:S(2)}) collective-permute-start(f32[2,2,128,1536]{3,2,1,0:T(8,128)} %pad_maximum_fusion.1), channel_id=1, source_target_pairs={{0,8},{1,9},{2,10},{3,11},{4,12},{5,13},{6,14},{7,15},{8,0},{9,1},... | collective-permute-start | bytes 9437192 | tf_op jit(solution)/shard_map/ppermute | solution.py:13
  171.3 2.3 copy-start.2
  171.3 2.7 copy-start.3
  174.0 139.6 %collective-permute-start.3 = (f32[2,2,128,1536]{3,2,1,0:T(8,128)}, f32[2,2,128,1536]{3,2,1,0:T(8,128)}, u32[]{:S(2)}, u32[]{:S(2)}) collective-permute-start(f32[2,2,128,1536]{3,2,1,0:T(8,128)} %pad_maximum_fusion.2), channel_id=1, source_target_pairs={{0,4},{1,5},{2,6},{3,7},{4,0},{5,1},{6,2},{7,3},{8,12},{9,13},{10,... | collective-permute-start | bytes 9437192 | tf_op jit(solution)/shard_map/ppermute | solution.py:13
  317.1 2.1 copy-start
  319.3 137.4 %collective-permute-start.4 = (f32[2,2,128,1536]{3,2,1,0:T(8,128)}, f32[2,2,128,1536]{3,2,1,0:T(8,128)}, u32[]{:S(2)}, u32[]{:S(2)}) collective-permute-start(f32[2,2,128,1536]{3,2,1,0:T(8,128)} %pad_maximum_fusion.3), channel_id=1, source_target_pairs={{0,2},{1,3},{2,0},{3,1},{4,6},{5,7},{6,4},{7,5},{8,10},{9,11},{10,... | collective-permute-start | bytes 9437192 | tf_op jit(solution)/shard_map/ppermute | solution.py:13
  459.8 2.1 copy-start.4
  459.8 2.7 copy-start.5
  462.5 69.5 %collective-permute-start.5 = (f32[2,2,128,1536]{3,2,1,0:T(8,128)}, f32[2,2,128,1536]{3,2,1,0:T(8,128)}, u32[]{:S(2)}, u32[]{:S(2)}) collective-permute-start(f32[2,2,128,1536]{3,2,1,0:T(8,128)} %pad_maximum_fusion.4), channel_id=1, source_target_pairs={{0,1},{1,0},{2,3},{3,2},{4,5},{5,4},{6,7},{7,6},{8,9},{9,8},{10,11... | collective-permute-start | bytes 9437192 | tf_op jit(solution)/shard_map/ppermute | solution.py:13
  552.1 46.1 %collective-permute-start.6 = (f32[2,2,128,1024]{3,2,1,0:T(8,128)}, f32[2,2,128,1024]{3,2,1,0:T(8,128)}, u32[]{:S(2)}, u32[]{:S(2)}) collective-permute-start(f32[2,2,128,1024]{3,2,1,0:T(8,128)} %pad_maximum_fusion.5), channel_id=1, source_target_pairs={{0,1},{1,0},{2,3},{3,2},{4,5},{5,4},{6,7},{7,6},{8,9},{9,8},{10,11... | collective-permute-start | bytes 6291464 | tf_op jit(solution)/shard_map/ppermute | solution.py:13
  600.3 1.0 copy-start.6
  602.7 91.7 %collective-permute-start.7 = (f32[2,2,128,1024]{3,2,1,0:T(8,128)}, f32[2,2,128,1024]{3,2,1,0:T(8,128)}, u32[]{:S(2)}, u32[]{:S(2)}) collective-permute-start(f32[2,2,128,1024]{3,2,1,0:T(8,128)} %pad_maximum_fusion.6), channel_id=1, source_target_pairs={{0,2},{1,3},{2,0},{3,1},{4,6},{5,7},{6,4},{7,5},{8,10},{9,11},{10,... | collective-permute-start | bytes 6291464 | tf_op jit(solution)/shard_map/ppermute | solution.py:13
  696.8 1.0 copy-start.7
  696.8 1.3 copy-start.8
  698.1 96.0 %collective-permute-start.8 = (f32[2,2,128,1024]{3,2,1,0:T(8,128)S(1)}, f32[2,2,128,1024]{3,2,1,0:T(8,128)}, u32[]{:S(2)}, u32[]{:S(2)}) collective-permute-start(f32[2,2,128,1024]{3,2,1,0:T(8,128)S(1)} %pad_maximum_fusion.7), channel_id=1, source_target_pairs={{0,4},{1,5},{2,6},{3,7},{4,0},{5,1},{6,2},{7,3},{8,12},{9,13},{10,... | collective-permute-start | bytes 6291464 | tf_op jit(solution)/shard_map/ppermute | solution.py:13
  798.3 47.3 %collective-permute-start.9 = (f32[2,2,128,1024]{3,2,1,0:T(8,128)}, f32[2,2,128,1024]{3,2,1,0:T(8,128)}, u32[]{:S(2)}, u32[]{:S(2)}) collective-permute-start(f32[2,2,128,1024]{3,2,1,0:T(8,128)} %pad_maximum_fusion.8), channel_id=1, source_target_pairs={{0,8},{1,9},{2,10},{3,11},{4,12},{5,13},{6,14},{7,15},{8,0},{9,1},... | collective-permute-start | bytes 6291464 | tf_op jit(solution)/shard_map/ppermute | solution.py:13
  847.8 48.2 %collective-permute-start.10 = (f32[2,2,128,1024]{3,2,1,0:T(8,128)S(1)}, f32[2,2,128,1024]{3,2,1,0:T(8,128)S(1)}, u32[]{:S(2)}, u32[]{:S(2)}) collective-permute-start(f32[2,2,128,1024]{3,2,1,0:T(8,128)S(1)} %pad_maximum_fusion.9), channel_id=1, source_target_pairs={{0,16},{1,17},{2,18},{3,19},{4,20},{5,21},{6,22},{7,23},{8,24},{9,... | collective-permute-start | bytes 6291464 | tf_op jit(solution)/shard_map/ppermute | solution.py:13
  896.6 1.1 copy-start.10
  896.6 1.2 copy-start.14
  896.6 1.2 copy-start.17
  896.7 1.2 copy-start.18
  975.7 6.5 collective-permute-start.11
Sparse Core Ops, SparseCore 0:
  981.2 60.1 all-reduce.3
where the time goes:
time: 1050 us
  waiting for transfers between devices  860 us (82%)
  blocking collectives  75.3 us (7%)
  other arithmetic  50.7 us (5%)
  starting transfers between devices  25.6 us (2%)
  between operations  15.3 us (1%)
  matrix products  14.2 us (1%)
    ppermute x10, waiting for transfers between devices, swapped(): return lax.ppermute(value, axis, pairs)  797 us
    psum x1, blocking collectives, per_device(): short_sum, skip_sum = lax.psum((short_part, skip_part), ('dp', 'ctx'))  75.3 us
    psum x1, waiting for transfers between devices, per_device(): filter_sum = lax.psum(filter_part, 'dp')  57.8 us
  transfers between devices with their start and end apart: 13, of which 13 were waited for; matrix products, arithmetic and copies ran while one was open for 0% of the time, Pallas kernels for 0%

commit v1 on v0

--- a/solution.py
+++ b/solution.py
@@ -175,7 +175,7 @@
     short_part = jnp.stack(short_rows)
     skip_part = jnp.sum(dconv * gated, axis=0)
     scale = 1.0 / math.sqrt(lax.axis_size("dp") * parts_count * tokens)
-    filter_sum = lax.psum(filter_part, "dp")
+    filter_sum = jnp.sum(lax.all_gather(filter_part, "dp"), axis=0)
     short_sum, skip_sum = lax.psum((short_part, skip_part), ("dp", "ctx"))
     return (layer_out, grad_features, short_sum * scale, filter_sum * scale, skip_sum * scale)
 

time: 1050 us -> 992 us (0.945)
  waiting for transfers between devices: 860 us -> 802 us
    psum x1 -> x0, waiting for transfers between devices: 57.8 us -> none  [per_device(): filter_sum = lax.psum(filter_part, 'dp')]
  transfers between devices with their start and end apart: 13 -> 13, of which waited for: 13 -> 11; matrix products, arithmetic and copies ran while one was open for 0% -> 0% of each run, Pallas kernels for 0% -> 0%
where the time goes in v1:
time: 992 us; the launch traced here: 990 us
  waiting for transfers between devices  802 us (81%)
  blocking collectives  75 us (8%)
  other arithmetic  51.6 us (5%)
  starting transfers between devices  24.2 us (2%)
  between operations  15.3 us (2%)
  matrix products  14.2 us (1%)
    ppermute x10, waiting for transfers between devices, swapped(): return lax.ppermute(value, axis, pairs)  797 us
    psum x1, blocking collectives, per_device(): short_sum, skip_sum = lax.psum((short_part, skip_part), ('dp', 'ctx'))  75 us
  transfers between devices with their start and end apart: 13, of which 11 were waited for; matrix products, arithmetic and copies ran while one was open for 0% of the time, Pallas kernels for 0%

profile of v1, /device:TPU:2, one launch (start us, length us, event | category | flops | bytes accessed | tf_op | source)
XLA Modules:
  0.0 990.3 jit_solution(6829172601875964276)
XLA Ops:
  7.2 0.7 slice_bitcast_fusion.20
  8.0 3.8 collective-permute-start
  11.8 1.3 slice_reduce_fusion.6
  13.2 4.3 collective-permute-done
  17.5 1.1 maximum_convert_fusion
  18.6 0.6 multiply_add_fusion.10
  19.6 1.0 copy-done.15
  21.3 0.5 copy-done.11
  22.0 1.9 pad_maximum_fusion
  23.9 2.4 collective-permute-start.1
  26.5 68.2 %collective-permute-done.1 = f32[2,2,128,1536]{3,2,1,0:T(8,128)} collective-permute-done((f32[2,2,128,1536]{3,2,1,0:T(8,128)}, f32[2,2,128,1536]{3,2,1,0:T(8,128)}, u32[]{:S(2)}, u32[]{:S(2)}) %collective-permute-start.1) | collective-permute-done | bytes 3145760 | tf_op jit(solution)/shard_map/ppermute | solution.py:13
  94.7 3.0 multiply_subtract_fusion.4
  97.7 2.0 pad_maximum_fusion.1
  100.3 67.9 %collective-permute-done.2 = f32[2,2,128,1536]{3,2,1,0:T(8,128)} collective-permute-done((f32[2,2,128,1536]{3,2,1,0:T(8,128)}, f32[2,2,128,1536]{3,2,1,0:T(8,128)}, u32[]{:S(2)}, u32[]{:S(2)}) %collective-permute-start.2) | collective-permute-done | bytes 3145760 | tf_op jit(solution)/shard_map/ppermute | solution.py:13
  168.2 3.1 multiply_subtract_fusion.3
  171.3 2.1 pad_maximum_fusion.2
  174.0 4.0 collective-permute-start.3
  178.1 135.4 %collective-permute-done.3 = f32[2,2,128,1536]{3,2,1,0:T(8,128)} collective-permute-done((f32[2,2,128,1536]{3,2,1,0:T(8,128)}, f32[2,2,128,1536]{3,2,1,0:T(8,128)}, u32[]{:S(2)}, u32[]{:S(2)}) %collective-permute-start.3) | collective-permute-done | bytes 3145760 | tf_op jit(solution)/shard_map/ppermute | solution.py:13
  313.5 3.6 multiply_subtract_fusion.2
  317.1 2.1 pad_maximum_fusion.3
  319.4 137.3 %collective-permute-done.4 = f32[2,2,128,1536]{3,2,1,0:T(8,128)} collective-permute-done((f32[2,2,128,1536]{3,2,1,0:T(8,128)}, f32[2,2,128,1536]{3,2,1,0:T(8,128)}, u32[]{:S(2)}, u32[]{:S(2)}) %collective-permute-start.4) | collective-permute-done | bytes 3145760 | tf_op jit(solution)/shard_map/ppermute | solution.py:13
  456.7 3.1 multiply_add_fusion.1
  459.8 2.0 pad_maximum_fusion.4
  461.9 0.6 copy-done.5
  462.6 69.4 %collective-permute-done.5 = f32[2,2,128,1536]{3,2,1,0:T(8,128)} collective-permute-done((f32[2,2,128,1536]{3,2,1,0:T(8,128)}, f32[2,2,128,1536]{3,2,1,0:T(8,128)}, u32[]{:S(2)}, u32[]{:S(2)}) %collective-permute-start.5) | collective-permute-done | bytes 3145760 | tf_op jit(solution)/shard_map/ppermute | solution.py:13
  532.0 3.5 fusion.2
  535.5 2.0 fusion.32
  537.5 2.0 fusion.33
  539.4 2.0 convolution_add_fusion
  541.4 2.0 convolution_subtract_fusion
  543.4 0.4 subtract_subtract_fusion
  544.0 1.5 fusion.24
  545.6 1.7 fusion.23
  547.3 1.5 convolution_add_fusion.1
  548.8 1.5 convolution_subtract_fusion.1
  550.6 1.5 pad_maximum_fusion.5
  552.4 45.8 %collective-permute-done.6 = f32[2,2,128,1024]{3,2,1,0:T(8,128)} collective-permute-done((f32[2,2,128,1024]{3,2,1,0:T(8,128)}, f32[2,2,128,1024]{3,2,1,0:T(8,128)}, u32[]{:S(2)}, u32[]{:S(2)}) %collective-permute-start.6) | collective-permute-done | bytes 2097184 | tf_op jit(solution)/shard_map/ppermute | solution.py:13
  598.2 2.0 multiply_add_fusion.8
  600.5 0.8 copy-done.6
  601.2 1.5 pad_maximum_fusion.6
  602.7 2.1 collective-permute-start.7
  604.8 89.6 %collective-permute-done.7 = f32[2,2,128,1024]{3,2,1,0:T(8,128)} collective-permute-done((f32[2,2,128,1024]{3,2,1,0:T(8,128)}, f32[2,2,128,1024]{3,2,1,0:T(8,128)}, u32[]{:S(2)}, u32[]{:S(2)}) %collective-permute-start.7) | collective-permute-done | bytes 2097184 | tf_op jit(solution)/shard_map/ppermute | solution.py:13
  694.5 2.3 multiply_add_fusion.7
  697.0 0.8 copy-done.7
  698.1 3.7 collective-permute-start.8
  701.8 92.3 %collective-permute-done.8 = f32[2,2,128,1024]{3,2,1,0:T(8,128)} collective-permute-done((f32[2,2,128,1024]{3,2,1,0:T(8,128)S(1)}, f32[2,2,128,1024]{3,2,1,0:T(8,128)}, u32[]{:S(2)}, u32[]{:S(2)}) %collective-permute-start.8) | collective-permute-done | bytes 2097184 | tf_op jit(solution)/shard_map/ppermute | solution.py:13
  794.1 2.7 multiply_add_fusion.6
  796.8 1.5 pad_maximum_fusion.8
  798.3 0.9 collective-permute-start.9
  799.2 46.3 %collective-permute-done.9 = f32[2,2,128,1024]{3,2,1,0:T(8,128)} collective-permute-done((f32[2,2,128,1024]{3,2,1,0:T(8,128)}, f32[2,2,128,1024]{3,2,1,0:T(8,128)}, u32[]{:S(2)}, u32[]{:S(2)}) %collective-permute-start.9) | collective-permute-done | bytes 2097184 | tf_op jit(solution)/shard_map/ppermute | solution.py:13
  845.5 2.0 multiply_subtract_fusion.5
  847.8 3.2 collective-permute-start.10
  851.0 45.0 %collective-permute-done.10 = f32[2,2,128,1024]{3,2,1,0:T(8,128)S(1)} collective-permute-done((f32[2,2,128,1024]{3,2,1,0:T(8,128)S(1)}, f32[2,2,128,1024]{3,2,1,0:T(8,128)S(1)}, u32[]{:S(2)}, u32[]{:S(2)}) %collective-permute-start.10) | collective-permute-done | bytes 2097184 | tf_op jit(solution)/shard_map/ppermute | solution.py:13
  896.0 0.6 fusion.12
  896.9 0.9 copy-done.10
  897.8 1.0 convert_multiply_fusion
  898.8 0.7 multiply_reduce_fusion
  899.7 3.4 collective-permute-start.11
  903.2 75.0 %all-reduce.1 = (f32[7,1536]{1,0:T(8,128)S(1)}, f32[512]{0:T(512)S(1)}) all-reduce(f32[7,1536]{1,0:T(8,128)S(1)} %stack.165, f32[512]{0:T(512)S(1)} %get-tuple-element.21), channel_id=1, replica_groups=mesh['dp'=8,'ctx'=32] {'dp','ctx'}, use_global_device_ids=true, to_apply=%region_7.8 | all-reduce | flops 11264 | bytes 90112 | tf_op jit(solution)/shard_map/psum | solution.py:179
  978.2 0.6 broadcast_multiply_fusion.1
  978.8 0.6 broadcast_multiply_fusion.2
  979.5 1.4 fusion.41
  980.9 1.8 reduce_sum.88
  982.7 0.7 broadcast_multiply_fusion
  (63 shorter events, 4.6 us)
Async XLA Ops:
  7.2 973.7 %all-gather.3.cloned.1.call-start = ((), (), s32[]{:S(2)}) async-start(), calls=%async_computation | async-start | bytes 2359296 | tf_op jit(solution)/shard_map/all_gather | solution.py:178
  8.0 9.5 collective-permute-start
  18.6 0.9 copy-start.16
  19.5 1.4 copy-start.9
  19.5 1.1 copy-start.15
  19.6 1.3 copy-start.13
  20.9 0.9 copy-start.11
  20.9 1.1 copy-start.12
  23.9 70.8 %collective-permute-start.1 = (f32[2,2,128,1536]{3,2,1,0:T(8,128)}, f32[2,2,128,1536]{3,2,1,0:T(8,128)}, u32[]{:S(2)}, u32[]{:S(2)}) collective-permute-start(f32[2,2,128,1536]{3,2,1,0:T(8,128)} %pad_maximum_fusion), channel_id=1, source_target_pairs={{0,16},{1,17},{2,18},{3,19},{4,20},{5,21},{6,22},{7,23},{8,24},{9,... | collective-permute-start | bytes 9437192 | tf_op jit(solution)/shard_map/ppermute | solution.py:13
  97.7 2.1 copy-start.1
  99.8 68.4 %collective-permute-start.2 = (f32[2,2,128,1536]{3,2,1,0:T(8,128)}, f32[2,2,128,1536]{3,2,1,0:T(8,128)}, u32[]{:S(2)}, u32[]{:S(2)}) collective-permute-start(f32[2,2,128,1536]{3,2,1,0:T(8,128)} %pad_maximum_fusion.1), channel_id=1, source_target_pairs={{0,8},{1,9},{2,10},{3,11},{4,12},{5,13},{6,14},{7,15},{8,0},{9,1},... | collective-permute-start | bytes 9437192 | tf_op jit(solution)/shard_map/ppermute | solution.py:13
  171.3 2.3 copy-start.2
  171.3 2.7 copy-start.3
  174.0 139.6 %collective-permute-start.3 = (f32[2,2,128,1536]{3,2,1,0:T(8,128)}, f32[2,2,128,1536]{3,2,1,0:T(8,128)}, u32[]{:S(2)}, u32[]{:S(2)}) collective-permute-start(f32[2,2,128,1536]{3,2,1,0:T(8,128)} %pad_maximum_fusion.2), channel_id=1, source_target_pairs={{0,4},{1,5},{2,6},{3,7},{4,0},{5,1},{6,2},{7,3},{8,12},{9,13},{10,... | collective-permute-start | bytes 9437192 | tf_op jit(solution)/shard_map/ppermute | solution.py:13
  317.1 2.1 copy-start
  319.3 137.4 %collective-permute-start.4 = (f32[2,2,128,1536]{3,2,1,0:T(8,128)}, f32[2,2,128,1536]{3,2,1,0:T(8,128)}, u32[]{:S(2)}, u32[]{:S(2)}) collective-permute-start(f32[2,2,128,1536]{3,2,1,0:T(8,128)} %pad_maximum_fusion.3), channel_id=1, source_target_pairs={{0,2},{1,3},{2,0},{3,1},{4,6},{5,7},{6,4},{7,5},{8,10},{9,11},{10,... | collective-permute-start | bytes 9437192 | tf_op jit(solution)/shard_map/ppermute | solution.py:13
  459.8 2.1 copy-start.4
  459.8 2.7 copy-start.5
  462.5 69.5 %collective-permute-start.5 = (f32[2,2,128,1536]{3,2,1,0:T(8,128)}, f32[2,2,128,1536]{3,2,1,0:T(8,128)}, u32[]{:S(2)}, u32[]{:S(2)}) collective-permute-start(f32[2,2,128,1536]{3,2,1,0:T(8,128)} %pad_maximum_fusion.4), channel_id=1, source_target_pairs={{0,1},{1,0},{2,3},{3,2},{4,5},{5,4},{6,7},{7,6},{8,9},{9,8},{10,11... | collective-permute-start | bytes 9437192 | tf_op jit(solution)/shard_map/ppermute | solution.py:13
  552.1 46.1 %collective-permute-start.6 = (f32[2,2,128,1024]{3,2,1,0:T(8,128)}, f32[2,2,128,1024]{3,2,1,0:T(8,128)}, u32[]{:S(2)}, u32[]{:S(2)}) collective-permute-start(f32[2,2,128,1024]{3,2,1,0:T(8,128)} %pad_maximum_fusion.5), channel_id=1, source_target_pairs={{0,1},{1,0},{2,3},{3,2},{4,5},{5,4},{6,7},{7,6},{8,9},{9,8},{10,11... | collective-permute-start | bytes 6291464 | tf_op jit(solution)/shard_map/ppermute | solution.py:13
  600.3 1.0 copy-start.6
  602.7 91.7 %collective-permute-start.7 = (f32[2,2,128,1024]{3,2,1,0:T(8,128)}, f32[2,2,128,1024]{3,2,1,0:T(8,128)}, u32[]{:S(2)}, u32[]{:S(2)}) collective-permute-start(f32[2,2,128,1024]{3,2,1,0:T(8,128)} %pad_maximum_fusion.6), channel_id=1, source_target_pairs={{0,2},{1,3},{2,0},{3,1},{4,6},{5,7},{6,4},{7,5},{8,10},{9,11},{10,... | collective-permute-start | bytes 6291464 | tf_op jit(solution)/shard_map/ppermute | solution.py:13
  696.8 1.0 copy-start.7
  696.8 1.3 copy-start.8
  698.1 96.0 %collective-permute-start.8 = (f32[2,2,128,1024]{3,2,1,0:T(8,128)S(1)}, f32[2,2,128,1024]{3,2,1,0:T(8,128)}, u32[]{:S(2)}, u32[]{:S(2)}) collective-permute-start(f32[2,2,128,1024]{3,2,1,0:T(8,128)S(1)} %pad_maximum_fusion.7), channel_id=1, source_target_pairs={{0,4},{1,5},{2,6},{3,7},{4,0},{5,1},{6,2},{7,3},{8,12},{9,13},{10,... | collective-permute-start | bytes 6291464 | tf_op jit(solution)/shard_map/ppermute | solution.py:13
  798.3 47.3 %collective-permute-start.9 = (f32[2,2,128,1024]{3,2,1,0:T(8,128)}, f32[2,2,128,1024]{3,2,1,0:T(8,128)}, u32[]{:S(2)}, u32[]{:S(2)}) collective-permute-start(f32[2,2,128,1024]{3,2,1,0:T(8,128)} %pad_maximum_fusion.8), channel_id=1, source_target_pairs={{0,8},{1,9},{2,10},{3,11},{4,12},{5,13},{6,14},{7,15},{8,0},{9,1},... | collective-permute-start | bytes 6291464 | tf_op jit(solution)/shard_map/ppermute | solution.py:13
  847.8 48.2 %collective-permute-start.10 = (f32[2,2,128,1024]{3,2,1,0:T(8,128)S(1)}, f32[2,2,128,1024]{3,2,1,0:T(8,128)S(1)}, u32[]{:S(2)}, u32[]{:S(2)}) collective-permute-start(f32[2,2,128,1024]{3,2,1,0:T(8,128)S(1)} %pad_maximum_fusion.9), channel_id=1, source_target_pairs={{0,16},{1,17},{2,18},{3,19},{4,20},{5,21},{6,22},{7,23},{8,24},{9,... | collective-permute-start | bytes 6291464 | tf_op jit(solution)/shard_map/ppermute | solution.py:13
  896.6 1.1 copy-start.10
  896.6 1.2 copy-start.14
  896.6 1.2 copy-start.17
  896.7 1.2 copy-start.18
  899.7 79.7 %collective-permute-start.11 = (f32[6,1536]{1,0:T(8,128)S(1)}, f32[6,1536]{1,0:T(8,128)S(1)}, u32[]{:S(2)}, u32[]{:S(2)}) collective-permute-start(f32[6,1536]{1,0:T(8,128)S(1)} %slice.294), channel_id=1, source_target_pairs={{1,0},{2,1},{3,2},{4,3},{5,4},{6,5},{7,6},{8,7},{9,8},{10,9},{11,1... | collective-permute-start | bytes 110600 | tf_op jit(solution)/shard_map/ppermute | solution.py:19
Sparse Core Ops, SparseCore 0:
  899.0 27.2 all-gather.2
